TPU v7x, 32 devices: a whole 2x2x4 slice. The times are simulated.
32 devices in a mesh: snap: 8 (over z, x), feat: 4 (over y, core).
Axes of the slice: x: 2, y: 2, z: 4, core: 2. Of those that a mesh axis runs over, the one named last changes fastest.
Arguments:
- node_features: bfloat16 [16, 512, 256], P('snap', None, 'feat'), may hold values from -6 to 6
- tile_rows: int32 [16, 8], P('snap'), may hold values from 0 to 3
- tile_cols: int32 [16, 8], P('snap'), may hold values from 0 to 3, as said below
- tile_counts: int32 [16], P('snap'), may hold values from 4 to 8, as said below
- tile_values: bfloat16 [16, 8, 128, 128], P('snap'), may hold values from -0.5 to 0.5
- layer_one: bfloat16 [256, 256], replicated, may hold values from -0.375 to 0.375
- layer_two: bfloat16 [256, 256], replicated, may hold values from -0.375 to 0.375
- query_weight: bfloat16 [256, 256], replicated, may hold values from -1.25 to 1.25
- key_weight: bfloat16 [256, 256], replicated, may hold values from -1.25 to 1.25
- value_weight: bfloat16 [256, 256], replicated, may hold values from -0.375 to 0.375
- out_weight: bfloat16 [256, 256], replicated, may hold values from -0.375 to 0.375
Outputs:
- evolved: bfloat16 [16, 512, 256], P('snap', None, 'feat')
Inputs may be any that keep to these rules, and one draw needn't show every extreme that they name: `tile_cols`: block columns of the tile slots; a coordinate pair may be listed more than once, and such tiles add. `tile_counts`: some snapshot uses all 8 slots.
All inputs are finite; a program needn't handle non-finite values.
Results may differ from a plain program's by a relative error of at most 0.02.
The roundings to bfloat16 on the way count: a program that leaves them out, or rounds other values in their place, can miss the bound.
Values may be sent and summed in bfloat16 or wider, within the bound.
A program may use at most 64 MiB of HBM per device.

v0:
```python
import jax
import jax.numpy as jnp
from jax import lax
from jax.sharding import PartitionSpec as P

HEADS = 8
masked_score = -1e30


def spread_padded(features, tile_block, block_rows, block_cols, slot_count):
    vert_count, feat_width = features.shape
    tile_side = tile_block.shape[1]
    slot_total = tile_block.shape[0]
    block_count = vert_count // tile_side
    blocked = features.reshape(block_count, tile_side, feat_width)
    picked_blocks = blocked[block_cols]
    live_slots = jnp.arange(slot_total, dtype=jnp.int32) < slot_count
    products = jnp.einsum(
        "irc,icf->irf", tile_block, picked_blocks, preferred_element_type=jnp.float32
    )
    products = products * live_slots.astype(jnp.float32)[:, None, None]
    membership = (
        (block_rows[None, :] == jnp.arange(block_count, dtype=jnp.int32)[:, None])
        & live_slots[None, :]
    ).astype(jnp.float32)
    summed = jnp.dot(
        membership,
        products.reshape(slot_total, tile_side * feat_width),
        precision=lax.Precision.HIGHEST,
    )
    return summed.reshape(vert_count, feat_width).astype(jnp.bfloat16)


def attend_local(hidden, query_weight, key_weight, value_weight, out_weight):
    snaps, verts, model_width = hidden.shape
    head_dim = model_width // HEADS
    flat = hidden.reshape(snaps * verts, model_width)

    def project(weight):
        return (
            jnp.dot(flat, weight, preferred_element_type=jnp.float32)
            .astype(jnp.bfloat16)
            .reshape(snaps, verts, HEADS, head_dim)
        )

    query_heads = project(query_weight)
    key_heads = project(key_weight)
    value_heads = project(value_weight)
    scores = jnp.einsum(
        "tvhd,uvhd->vhtu", query_heads, key_heads, preferred_element_type=jnp.float32
    ) * head_dim ** (-0.5)
    causal = (
        jnp.arange(snaps, dtype=jnp.int32)[:, None] >= jnp.arange(snaps, dtype=jnp.int32)[None, :]
    )
    scores = jnp.where(causal, scores, masked_score)
    row_max = jnp.max(scores, axis=-1, keepdims=True)
    lifted = jnp.exp(scores - row_max)
    weights = (lifted / jnp.sum(lifted, axis=-1, keepdims=True)).astype(jnp.bfloat16)
    context = jnp.einsum(
        "vhtu,uvhd->tvhd", weights, value_heads, preferred_element_type=jnp.float32
    ).astype(jnp.bfloat16)
    context = context.reshape(snaps * verts, model_width)
    result = flat.astype(jnp.float32) + jnp.dot(
        context, out_weight, preferred_element_type=jnp.float32
    )
    return result.astype(jnp.bfloat16).reshape(snaps, verts, model_width)


def on_device(
    node_features,
    tile_rows,
    tile_cols,
    tile_counts,
    tile_values,
    layer_one,
    layer_two,
    query_weight,
    key_weight,
    value_weight,
    out_weight,
):
    snap_dev, vert_count, feat_width = node_features.shape
    feat_index = lax.axis_index("feat")

    def spread_all(features):
        spread_pieces = []
        for snapshot in range(snap_dev):
            spread_pieces.append(
                spread_padded(
                    features[snapshot],
                    tile_values[snapshot],
                    tile_rows[snapshot],
                    tile_cols[snapshot],
                    tile_counts[snapshot],
                )
            )
        return jnp.stack(spread_pieces, axis=0)

    def convolve(features, weight):
        spread_rows = spread_all(features).reshape(snap_dev * vert_count, feat_width)
        own_columns = lax.dynamic_slice_in_dim(weight, feat_index * feat_width, feat_width, 1)
        mixed_sum = jnp.dot(
            lax.all_gather(spread_rows, "feat", axis=1, tiled=True),
            own_columns,
            preferred_element_type=jnp.float32,
        )
        mixed_sum = mixed_sum.reshape(snap_dev, vert_count, feat_width)
        return (features.astype(jnp.float32) + jnp.maximum(mixed_sum, 0.0)).astype(jnp.bfloat16)

    hidden_one = convolve(node_features, layer_one)
    hidden_two = convolve(hidden_one, layer_two)
    vertex_rows = lax.all_to_all(
        lax.all_to_all(hidden_two, "snap", split_axis=1, concat_axis=0, tiled=True),
        "feat",
        split_axis=1,
        concat_axis=2,
        tiled=True,
    )
    attended = attend_local(vertex_rows, query_weight, key_weight, value_weight, out_weight)
    return lax.all_to_all(
        lax.all_to_all(attended, "feat", split_axis=2, concat_axis=1, tiled=True),
        "snap",
        split_axis=0,
        concat_axis=1,
        tiled=True,
    )


def solution(mesh):
    placed = (
        P("snap", None, "feat"),
        P("snap", None),
        P("snap", None),
        P("snap"),
        P("snap", None, None, None),
        P(),
        P(),
        P(),
        P(),
        P(),
        P(),
    )
    return jax.shard_map(
        on_device, mesh=mesh, in_specs=placed, out_specs=P("snap", None, "feat"), check_vma=False
    )
```

profile of v0, /device:TPU:0, one launch (start us, length us, event | category | flops | bytes accessed | tf_op | source)
XLA Modules:
  0.0 81.3 jit_solution(12368943352257759503)
XLA Ops:
  0.0 0.7 copy-done.9
  0.7 0.9 %fusion.47 = (bf16[1,512,64]{1,2,0:T(8,128)(2,1)S(1)}, bf16[1,512,64]{1,2,0:T(8,128)(2,1)S(1)}) fusion(bf16[2,512,64]{1,2,0:T(8,128)(2,1)} %param.11), kind=kLoop, calls=%fused_computation.79 | loop fusion | bytes 262144 | tf_op jit(solution)/shard_map/slice | solution.py:90
  1.7 0.6 copy-done.8
  2.4 0.6 fusion.48
  3.0 0.6 iota_compare_fusion.4
  3.6 0.6 gather_fusion
  4.2 0.3 fusion.8
  4.5 0.2 copy.104
  4.7 0.2 reshape.167
  4.9 0.5 copy-done.10
  5.4 0.2 convolution_convert_fusion.3
  5.9 0.6 iota_compare_fusion.3
  6.5 0.6 gather_fusion.1
  7.1 0.3 fusion.7
  7.4 0.2 copy.106
  7.6 0.2 reshape.168
  7.8 0.2 convolution_convert_fusion.2
  8.4 8.7 %all_gather.6 = bf16[1024,256]{0,1:T(8,128)(2,1)S(1)} all-gather(bf16[1024,64]{0,1:T(8,128)(2,1)S(1)} %copy.107), channel_id=1, replica_groups=mesh['snap'=8,'feat'=4] {'feat'}, dimensions={1}, use_global_device_ids=true | all-gather | bytes 655360 | tf_op jit(solution)/shard_map/all_gather | solution.py:103
  17.1 0.3 convolution_maximum_fusion.1
  17.4 0.6 copy-done.2
  18.1 0.6 gather_fusion.2
  18.6 0.3 fusion.6
  18.9 0.2 copy.110
  19.1 0.2 reshape.170
  19.3 0.2 convolution_convert_fusion.1
  19.8 0.6 gather_fusion.3
  20.4 0.3 fusion.5
  20.6 0.2 copy.112
  20.9 0.2 reshape.171
  21.0 0.2 convolution_convert_fusion
  21.7 7.4 %all_gather.7 = bf16[1024,256]{0,1:T(8,128)(2,1)S(1)} all-gather(bf16[1024,64]{0,1:T(8,128)(2,1)S(1)} %copy.113), channel_id=1, replica_groups=mesh['snap'=8,'feat'=4] {'feat'}, dimensions={1}, use_global_device_ids=true | all-gather | bytes 655360 | tf_op jit(solution)/shard_map/all_gather | solution.py:103
  29.1 0.3 convolution_maximum_fusion
  29.6 0.2 reshape.211
  29.9 13.1 %all_to_all.69 = bf16[8,2,4096]{2,1,0:T(2,128)(2,1)S(1)} all-to-all(bf16[8,2,4096]{2,1,0:T(2,128)(2,1)S(1)} %reshape.211), channel_id=1, replica_groups=mesh['snap'=8,'feat'=4] {'snap'}, dimensions={0} | all-to-all | bytes 262144 | tf_op jit(solution)/shard_map/all_to_all | solution.py:113
  43.0 0.2 reshape.212
  43.4 0.9 %reshape.213 = bf16[4,2,8192]{2,1,0:T(2,128)(2,1)} reshape(bf16[64,16,64]{2,1,0:T(8,128)(2,1)S(1)} %bitcast.111) | data formatting | bytes 262144
  44.3 3.3 %all-to-all-start.1 = ((bf16[4,2,8192]{2,1,0:T(2,128)(2,1)}), bf16[4,2,8192]{2,1,0:T(2,128)(2,1)S(1)}, u32[]{:S(2)}, u32[]{:S(2)}) async-start(bf16[4,2,8192]{2,1,0:T(2,128)(2,1)} %reshape.213), calls=%async_computation.1 | async-start | bytes 262144 | tf_op jit(solution)/shard_map/all_to_all | solution.py:112
  47.7 4.6 %all-to-all-done.1 = bf16[4,2,8192]{2,1,0:T(2,128)(2,1)S(1)} async-done(((bf16[4,2,8192]{2,1,0:T(2,128)(2,1)}), bf16[4,2,8192]{2,1,0:T(2,128)(2,1)S(1)}, u32[]{:S(2)}, u32[]{:S(2)}) %all-to-all-start.1) | async-done | bytes 131104 | tf_op jit(solution)/shard_map/all_to_all | solution.py:112
  52.2 0.2 reshape.214
  52.4 0.2 copy.120
  52.7 0.2 reshape.173
  52.9 0.7 copy-done.3
  53.6 0.2 convolution_convert_fusion.6
  53.8 0.2 reshape.175
  54.0 0.7 copy-done.4
  54.7 0.2 convolution_convert_fusion.5
  54.9 0.2 reshape.176
  55.1 0.7 copy-done.5
  55.9 0.2 reshape.174
  56.2 1.0 %fusion.49 = (f32[16,8,16]{2,1,0:T(8,128)S(1)}, f32[16,8,16,16]{2,3,1,0:T(8,128)S(1)}) fusion(bf16[16,16,8,32]{3,2,1,0:T(8,128)(2,1)S(1)} %reshape.176, bf16[16,16,8,32]{3,2,1,0:T(8,128)(2,1)S(1)} %reshape.175, pred[16,16]{0,1:T(8,128)(4,1)S(1)} %iota_compare_fusion), kind=kOutput, calls=%fused_computation.81 | convolution fusion | flops 2228239 | bytes 401664 | tf_op jit(solution)/shard_map/sub | solution.py:57
  57.2 0.5 fusion.4
  57.9 0.4 reshape.177
  58.3 0.5 copy-done.6
  58.8 0.2 fusion.9
  59.0 0.9 %copy.126 = bf16[16,16,256]{1,0,2:T(8,128)(2,1)S(1)} copy(bf16[16,16,256]{2,1,0:T(8,128)(2,1)S(1)} %bitcast.115) | data formatting | bytes 262144 | tf_op jit(solution)/shard_map/reshape | solution.py:66
  60.0 1.1 %reshape.215 = bf16[4,2,8192]{2,1,0:T(2,128)(2,1)S(1)} reshape(bf16[256,16,16]{2,1,0:T(8,128)(2,1)S(1)} %bitcast.102) | data formatting | bytes 262144
  61.0 7.0 %all_to_all.70 = bf16[4,2,8192]{2,1,0:T(2,128)(2,1)S(1)} all-to-all(bf16[4,2,8192]{2,1,0:T(2,128)(2,1)S(1)} %reshape.215), channel_id=1, replica_groups=mesh['snap'=8,'feat'=4] {'feat'}, dimensions={0} | all-to-all | bytes 262144 | tf_op jit(solution)/shard_map/all_to_all | solution.py:121
  68.0 0.7 reshape.216
  68.7 1.2 %copy.134 = bf16[16,16,4,64]{3,2,1,0:T(4,128)(2,1)S(1)} copy(bf16[16,16,4,64]{1,0,3,2:T(8,128)(2,1)S(1)} %bitcast.101) | data formatting | bytes 262144 | tf_op jit(solution)/shard_map/all_to_all | solution.py:121
  69.9 0.2 reshape.217
  70.2 9.9 %all_to_all.71 = bf16[8,2,4096]{2,1,0:T(2,128)(2,1)S(1)} all-to-all(bf16[8,2,4096]{2,1,0:T(2,128)(2,1)S(1)} %reshape.217), channel_id=1, replica_groups=mesh['snap'=8,'feat'=4] {'snap'}, dimensions={0} | all-to-all | bytes 262144 | tf_op jit(solution)/shard_map/all_to_all | solution.py:120
  80.0 0.2 reshape.218
  80.3 0.2 copy.129
  80.5 0.9 %all_to_all.64 = bf16[2,512,64]{1,2,0:T(8,128)(2,1)} reshape(bf16[2,8,64,64]{2,1,3,0:T(8,128)(2,1)S(1)} %copy.129) | data formatting | bytes 262144 | tf_op jit(solution)/shard_map/all_to_all | solution.py:120
  (43 shorter events, 2.0 us)
Async XLA Ops:
  0.0 17.1 %copy-start = (bf16[256,256]{1,0:T(8,128)(2,1)S(1)}, bf16[256,256]{1,0:T(8,128)(2,1)}, u32[]{:S(2)}) copy-start(bf16[256,256]{1,0:T(8,128)(2,1)} %param.16) | copy-start | bytes 393220
  0.0 0.7 copy-start.9
  0.7 3.5 %copy-start.1 = (bf16[2,8,128,128]{3,2,1,0:T(8,128)(2,1)S(1)}, bf16[2,8,128,128]{3,2,1,0:T(8,128)(2,1)}, u32[]{:S(2)}) copy-start(bf16[2,8,128,128]{3,2,1,0:T(8,128)(2,1)} %param.15) | copy-start | bytes 1572868
  1.7 0.7 copy-start.8
  4.7 0.7 copy-start.10
  17.1 0.9 %copy-start.2 = (bf16[2,512,64]{1,2,0:T(8,128)(2,1)S(1)}, bf16[2,512,64]{1,2,0:T(8,128)(2,1)}, u32[]{:S(2)}) copy-start(bf16[2,512,64]{1,2,0:T(8,128)(2,1)} %param.11) | copy-start | bytes 393220
  21.7 7.4 %copy-start.7 = (bf16[256,256]{1,0:T(8,128)(2,1)S(1)}, bf16[256,256]{1,0:T(8,128)(2,1)}, u32[]{:S(2)}) copy-start(bf16[256,256]{1,0:T(8,128)(2,1)} %param.17) | copy-start | bytes 393220
  44.3 7.9 %all-to-all-start.1 = ((bf16[4,2,8192]{2,1,0:T(2,128)(2,1)}), bf16[4,2,8192]{2,1,0:T(2,128)(2,1)S(1)}, u32[]{:S(2)}, u32[]{:S(2)}) async-start(bf16[4,2,8192]{2,1,0:T(2,128)(2,1)} %reshape.213), calls=%async_computation.1 | async-start | bytes 262144 | tf_op jit(solution)/shard_map/all_to_all | solution.py:112
  52.7 0.9 %copy-start.3 = (bf16[256,256]{1,0:T(8,128)(2,1)S(1)}, bf16[256,256]{1,0:T(8,128)(2,1)}, u32[]{:S(2)}) copy-start(bf16[256,256]{1,0:T(8,128)(2,1)} %param.18) | copy-start | bytes 393220
  53.8 0.9 %copy-start.4 = (bf16[256,256]{1,0:T(8,128)(2,1)S(1)}, bf16[256,256]{1,0:T(8,128)(2,1)}, u32[]{:S(2)}) copy-start(bf16[256,256]{1,0:T(8,128)(2,1)} %param.19) | copy-start | bytes 393220
  54.9 0.9 %copy-start.5 = (bf16[256,256]{1,0:T(8,128)(2,1)S(1)}, bf16[256,256]{1,0:T(8,128)(2,1)}, u32[]{:S(2)}) copy-start(bf16[256,256]{1,0:T(8,128)(2,1)} %param.20) | copy-start | bytes 393220
  57.9 0.9 %copy-start.6 = (bf16[256,256]{1,0:T(8,128)(2,1)S(1)}, bf16[256,256]{1,0:T(8,128)(2,1)}, u32[]{:S(2)}) copy-start(bf16[256,256]{1,0:T(8,128)(2,1)} %param.21) | copy-start | bytes 393220
where the time goes:
time: 81.8 us; the launch traced here: 81.3 us
  blocking collectives  46 us (56%)
  local copies, waits for them, and re-layouts  20.4 us (25%)
  matrix products  4.96 us (6%)
  waiting for transfers between devices  4.55 us (6%)
  starting transfers between devices  3.33 us (4%)
  other arithmetic  1.48 us (2%)
    all_gather x2, blocking collectives, convolve(): lax.all_gather(spread_rows, 'feat', axis=1, tiled=True)  16.1 us
    all_to_all x1, blocking collectives, on_device(): lax.all_to_all(hidden_two, 'snap', split_axis=1, concat_axis=0, tiled=True)  13.1 us
    all_to_all x1, blocking collectives, on_device(): lax.all_to_all(lax.all_to_all(attended, 'feat', split_axis=2, concat_axis...  9.86 us
    unnamed x30, local copies, waits for them, and re-layouts  8.75 us
    all_to_all x1, blocking collectives, on_device(): lax.all_to_all(attended, 'feat', split_axis=2, concat_axis=1, tiled=True)  6.99 us
    all_to_all x1, waiting for transfers between devices, on_device(): lax.all_to_all(lax.all_to_all(hidden_two, 'snap', split_axis=1, concat_ax...  4.55 us
    all_to_all x1, starting transfers between devices, on_device(): lax.all_to_all(lax.all_to_all(hidden_two, 'snap', split_axis=1, concat_ax...  3.33 us
    gather x4, local copies, waits for them, and re-layouts, spread_padded(): picked_blocks = blocked[block_cols]  2.29 us
  transfers between devices with their start and end apart: 1, of which 1 were waited for; matrix products, arithmetic and copies ran while one was open for 0% of the time, Pallas kernels for 0%

commit v1 on v0

--- a/solution.py
+++ b/solution.py
@@ -117,12 +117,20 @@
         tiled=True,
     )
     attended = attend_local(vertex_rows, query_weight, key_weight, value_weight, out_weight)
-    return lax.all_to_all(
-        lax.all_to_all(attended, "feat", split_axis=2, concat_axis=1, tiled=True),
-        "snap",
-        split_axis=0,
-        concat_axis=1,
-        tiled=True,
+    return jnp.concatenate(
+        lax.all_to_all(
+            jnp.stack(
+                jnp.split(
+                    lax.all_to_all(attended, "feat", split_axis=2, concat_axis=1, tiled=True),
+                    lax.axis_size("snap"),
+                    axis=0,
+                )
+            ),
+            "snap",
+            0,
+            0,
+        ),
+        axis=1,
     )
 
 

time: 81.8 us -> 82 us (level)
    all_to_all x2 -> x0, local copies, waits for them, and re-layouts: 1.07 us -> none  [on_device(): lax.all_to_all(lax.all_to_all(attended, 'feat', split_axis=2, concat_axis...]
    reshape x0 -> x2, local copies, waits for them, and re-layouts: none -> 1.07 us  [on_device(): jnp.concatenate(lax.all_to_all(jnp.stack(jnp.split(lax.all_to_all(attende...]
    unnamed x30 -> x37, local copies, waits for them, and re-layouts: 8.75 us -> 8.81 us
where the time goes in v1:
time: 82 us; the launch traced here: 81.5 us
  blocking collectives  46 us (56%)
  local copies, waits for them, and re-layouts  20.6 us (25%)
  matrix products  4.97 us (6%)
  waiting for transfers between devices  4.55 us (6%)
  starting transfers between devices  3.33 us (4%)
  other arithmetic  1.39 us (2%)
    all_gather x2, blocking collectives, convolve(): lax.all_gather(spread_rows, 'feat', axis=1, tiled=True)  16.1 us
    all_to_all x1, blocking collectives, on_device(): lax.all_to_all(hidden_two, 'snap', split_axis=1, concat_axis=0, tiled=True)  13.1 us
    all_to_all x1, blocking collectives, on_device(): lax.all_to_all(jnp.stack(jnp.split(lax.all_to_all(attended, 'feat', split...  9.85 us
    unnamed x37, local copies, waits for them, and re-layouts  8.81 us
    all_to_all x1, blocking collectives, on_device(): lax.all_to_all(attended, 'feat', split_axis=2, concat_axis=1, tiled=True)  6.99 us
    all_to_all x1, waiting for transfers between devices, on_device(): lax.all_to_all(lax.all_to_all(hidden_two, 'snap', split_axis=1, concat_ax...  4.55 us
    all_to_all x1, starting transfers between devices, on_device(): lax.all_to_all(lax.all_to_all(hidden_two, 'snap', split_axis=1, concat_ax...  3.33 us
    gather x4, local copies, waits for them, and re-layouts, spread_padded(): picked_blocks = blocked[block_cols]  2.29 us
  transfers between devices with their start and end apart: 1, of which 1 were waited for; matrix products, arithmetic and copies ran while one was open for 0% of the time, Pallas kernels for 0%

profile of v1, /device:TPU:0, one launch (start us, length us, event | category | flops | bytes accessed | tf_op | source)
XLA Modules:
  0.0 81.5 jit_solution(8275645558342450618)
XLA Ops:
  0.0 0.7 copy-done.9
  0.7 0.9 %fusion.48 = (bf16[1,512,64]{1,2,0:T(8,128)(2,1)S(1)}, bf16[1,512,64]{1,2,0:T(8,128)(2,1)S(1)}) fusion(bf16[2,512,64]{1,2,0:T(8,128)(2,1)} %param.11), kind=kLoop, calls=%fused_computation.88 | loop fusion | bytes 262144 | tf_op jit(solution)/shard_map/slice | solution.py:90
  1.7 0.6 copy-done.8
  2.4 0.6 fusion.49
  2.9 0.6 iota_compare_fusion.4
  3.6 0.6 gather_fusion
  4.2 0.3 fusion.8
  4.4 0.2 copy.133
  4.7 0.2 reshape.189
  4.9 0.5 copy-done.10
  5.3 0.2 convolution_convert_fusion.3
  5.8 0.5 iota_compare_fusion.3
  6.4 0.6 gather_fusion.1
  6.9 0.3 fusion.7
  7.2 0.2 copy.135
  7.4 0.2 reshape.190
  7.6 0.2 convolution_convert_fusion.2
  8.2 8.7 %all_gather.6 = bf16[1024,256]{0,1:T(8,128)(2,1)S(1)} all-gather(bf16[1024,64]{0,1:T(8,128)(2,1)S(1)} %copy.136), channel_id=1, replica_groups=mesh['snap'=8,'feat'=4] {'feat'}, dimensions={1}, use_global_device_ids=true | all-gather | bytes 655360 | tf_op jit(solution)/shard_map/all_gather | solution.py:103
  16.9 0.3 convolution_maximum_fusion.1
  17.2 0.6 copy-done.2
  17.9 0.6 gather_fusion.2
  18.5 0.3 fusion.6
  18.8 0.2 copy.139
  19.0 0.2 reshape.192
  19.2 0.2 convolution_convert_fusion.1
  19.6 0.6 gather_fusion.3
  20.2 0.3 fusion.5
  20.5 0.2 copy.141
  20.7 0.2 reshape.193
  20.9 0.2 convolution_convert_fusion
  21.5 7.4 %all_gather.7 = bf16[1024,256]{0,1:T(8,128)(2,1)S(1)} all-gather(bf16[1024,64]{0,1:T(8,128)(2,1)S(1)} %copy.142), channel_id=1, replica_groups=mesh['snap'=8,'feat'=4] {'feat'}, dimensions={1}, use_global_device_ids=true | all-gather | bytes 655360 | tf_op jit(solution)/shard_map/all_gather | solution.py:103
  29.0 0.3 convolution_maximum_fusion
  29.5 0.2 reshape.235
  29.7 13.1 %all_to_all.53 = bf16[8,2,4096]{2,1,0:T(2,128)(2,1)S(1)} all-to-all(bf16[8,2,4096]{2,1,0:T(2,128)(2,1)S(1)} %reshape.235), channel_id=1, replica_groups=mesh['snap'=8,'feat'=4] {'snap'}, dimensions={0} | all-to-all | bytes 262144 | tf_op jit(solution)/shard_map/all_to_all | solution.py:113
  42.8 0.2 reshape.236
  43.3 0.9 %reshape.237 = bf16[4,2,8192]{2,1,0:T(2,128)(2,1)} reshape(bf16[64,16,64]{2,1,0:T(8,128)(2,1)S(1)} %bitcast.116) | data formatting | bytes 262144
  44.2 3.3 %all-to-all-start.1 = ((bf16[4,2,8192]{2,1,0:T(2,128)(2,1)}), bf16[4,2,8192]{2,1,0:T(2,128)(2,1)S(1)}, u32[]{:S(2)}, u32[]{:S(2)}) async-start(bf16[4,2,8192]{2,1,0:T(2,128)(2,1)} %reshape.237), calls=%async_computation.1 | async-start | bytes 262144 | tf_op jit(solution)/shard_map/all_to_all | solution.py:112
  47.5 4.6 %all-to-all-done.1 = bf16[4,2,8192]{2,1,0:T(2,128)(2,1)S(1)} async-done(((bf16[4,2,8192]{2,1,0:T(2,128)(2,1)}), bf16[4,2,8192]{2,1,0:T(2,128)(2,1)S(1)}, u32[]{:S(2)}, u32[]{:S(2)}) %all-to-all-start.1) | async-done | bytes 131104 | tf_op jit(solution)/shard_map/all_to_all | solution.py:112
  52.1 0.2 reshape.238
  52.3 0.2 copy.149
  52.5 0.2 reshape.195
  52.7 0.7 copy-done.3
  53.4 0.2 convolution_convert_fusion.6
  53.6 0.2 reshape.197
  53.9 0.7 copy-done.4
  54.7 0.2 reshape.198
  55.0 0.7 copy-done.5
  55.6 0.2 convolution_convert_fusion.7
  55.8 0.2 reshape.196
  56.1 1.0 %fusion.50 = (f32[16,8,16]{2,1,0:T(8,128)S(1)}, f32[16,8,16,16]{2,3,1,0:T(8,128)S(1)}) fusion(bf16[16,16,8,32]{3,2,1,0:T(8,128)(2,1)S(1)} %reshape.198, bf16[16,16,8,32]{3,2,1,0:T(8,128)(2,1)S(1)} %reshape.197, pred[16,16]{0,1:T(8,128)(4,1)S(1)} %iota_compare_fusion), kind=kOutput, calls=%fused_computation.90 | convolution fusion | flops 2228239 | bytes 401664 | tf_op jit(solution)/shard_map/sub | solution.py:57
  57.1 0.5 fusion.4
  57.8 0.4 reshape.199
  58.1 0.5 copy-done.6
  58.7 0.2 fusion.9
  58.9 0.9 %copy.155 = bf16[16,16,256]{1,0,2:T(8,128)(2,1)S(1)} copy(bf16[16,16,256]{2,1,0:T(8,128)(2,1)S(1)} %bitcast.119) | data formatting | bytes 262144 | tf_op jit(solution)/shard_map/reshape | solution.py:66
  59.8 1.1 %reshape.239 = bf16[4,2,8192]{2,1,0:T(2,128)(2,1)S(1)} reshape(bf16[256,16,16]{2,1,0:T(8,128)(2,1)S(1)} %bitcast.107) | data formatting | bytes 262144
  60.9 7.0 %all_to_all.54 = bf16[4,2,8192]{2,1,0:T(2,128)(2,1)S(1)} all-to-all(bf16[4,2,8192]{2,1,0:T(2,128)(2,1)S(1)} %reshape.239), channel_id=1, replica_groups=mesh['snap'=8,'feat'=4] {'feat'}, dimensions={0} | all-to-all | bytes 262144 | tf_op jit(solution)/shard_map/all_to_all | solution.py:124
  67.9 0.7 reshape.240
  68.6 1.2 %copy.170 = bf16[16,16,4,64]{3,2,1,0:T(4,128)(2,1)S(1)} copy(bf16[16,16,4,64]{1,0,3,2:T(8,128)(2,1)S(1)} %bitcast.106) | data formatting | bytes 262144 | tf_op jit(solution)/shard_map/all_to_all | solution.py:124
  70.1 0.2 reshape.241
  70.3 9.9 %all_to_all.55 = bf16[8,2,4096]{2,1,0:T(2,128)(2,1)S(1)} all-to-all(bf16[8,2,4096]{2,1,0:T(2,128)(2,1)S(1)} %reshape.241), channel_id=1, replica_groups=mesh['snap'=8,'feat'=4] {'snap'}, dimensions={0} | all-to-all | bytes 262144 | tf_op jit(solution)/shard_map/all_to_all | solution.py:121
  80.2 0.2 reshape.242
  80.4 0.2 copy.165
  80.6 0.9 %reshape.202 = bf16[2,512,64]{1,2,0:T(8,128)(2,1)} reshape(bf16[2,8,64,64]{2,1,3,0:T(8,128)(2,1)S(1)} %copy.165) | data formatting | bytes 262144 | tf_op jit(solution)/shard_map/reshape | solution.py:120
  (59 shorter events, 2.2 us)
Async XLA Ops:
  0.0 16.9 %copy-start = (bf16[256,256]{1,0:T(8,128)(2,1)S(1)}, bf16[256,256]{1,0:T(8,128)(2,1)}, u32[]{:S(2)}) copy-start(bf16[256,256]{1,0:T(8,128)(2,1)} %param.16) | copy-start | bytes 393220
  0.0 0.7 copy-start.9
  0.7 3.4 %copy-start.1 = (bf16[2,8,128,128]{3,2,1,0:T(8,128)(2,1)S(1)}, bf16[2,8,128,128]{3,2,1,0:T(8,128)(2,1)}, u32[]{:S(2)}) copy-start(bf16[2,8,128,128]{3,2,1,0:T(8,128)(2,1)} %param.15) | copy-start | bytes 1572868
  1.7 0.7 copy-start.8
  4.7 0.7 copy-start.10
  16.9 0.9 %copy-start.2 = (bf16[2,512,64]{1,2,0:T(8,128)(2,1)S(1)}, bf16[2,512,64]{1,2,0:T(8,128)(2,1)}, u32[]{:S(2)}) copy-start(bf16[2,512,64]{1,2,0:T(8,128)(2,1)} %param.11) | copy-start | bytes 393220
  21.5 7.4 %copy-start.7 = (bf16[256,256]{1,0:T(8,128)(2,1)S(1)}, bf16[256,256]{1,0:T(8,128)(2,1)}, u32[]{:S(2)}) copy-start(bf16[256,256]{1,0:T(8,128)(2,1)} %param.17) | copy-start | bytes 393220
  44.2 7.9 %all-to-all-start.1 = ((bf16[4,2,8192]{2,1,0:T(2,128)(2,1)}), bf16[4,2,8192]{2,1,0:T(2,128)(2,1)S(1)}, u32[]{:S(2)}, u32[]{:S(2)}) async-start(bf16[4,2,8192]{2,1,0:T(2,128)(2,1)} %reshape.237), calls=%async_computation.1 | async-start | bytes 262144 | tf_op jit(solution)/shard_map/all_to_all | solution.py:112
  52.5 0.9 %copy-start.3 = (bf16[256,256]{1,0:T(8,128)(2,1)S(1)}, bf16[256,256]{1,0:T(8,128)(2,1)}, u32[]{:S(2)}) copy-start(bf16[256,256]{1,0:T(8,128)(2,1)} %param.18) | copy-start | bytes 393220
  53.6 0.9 %copy-start.4 = (bf16[256,256]{1,0:T(8,128)(2,1)S(1)}, bf16[256,256]{1,0:T(8,128)(2,1)}, u32[]{:S(2)}) copy-start(bf16[256,256]{1,0:T(8,128)(2,1)} %param.19) | copy-start | bytes 393220
  54.7 0.9 %copy-start.5 = (bf16[256,256]{1,0:T(8,128)(2,1)S(1)}, bf16[256,256]{1,0:T(8,128)(2,1)}, u32[]{:S(2)}) copy-start(bf16[256,256]{1,0:T(8,128)(2,1)} %param.20) | copy-start | bytes 393220
  57.8 0.9 %copy-start.6 = (bf16[256,256]{1,0:T(8,128)(2,1)S(1)}, bf16[256,256]{1,0:T(8,128)(2,1)}, u32[]{:S(2)}) copy-start(bf16[256,256]{1,0:T(8,128)(2,1)} %param.21) | copy-start | bytes 393220
